TPU v7x, 256 devices: a whole 4x4x8 slice. The times are simulated.
256 devices in a mesh: gx: 8 (over x, core), gy: 32 (over y, z).
Axes of the slice: x: 4, y: 4, z: 8, core: 2. Of those that a mesh axis runs over, the one named last changes fastest.
Arguments:
- features: float32 [64, 524288], P(None, ('gx', 'gy')), may hold values from -6 to 6
- cotangent: float32 [64, 524288], P(None, ('gx', 'gy')), may hold values from -6 to 6
- edge_src: int32 [8, 524288], P(None, ('gx', 'gy')), may hold values from 0 to 2559
- send_rows: int32 [4, 32768], P(None, ('gx', 'gy')), may hold values from 0 to 2047
- fine_to_coarse: int32 [524288], P(('gx', 'gy')), may hold values from 0 to 2047
- coarse_to_fine: int32 [524288], P(('gx', 'gy')), may hold values from 0 to 2047
- coarse_edges: int32 [2, 8192], replicated, may hold values from 0 to 2047
- edge_in: float32 [64, 128], replicated, may hold values from -0.5 to 0.5
- edge_out: float32 [64, 64], replicated, may hold values from -0.75 to 0.75
- node_in: float32 [64, 128], replicated, may hold values from -0.5 to 0.5
- node_out: float32 [64, 64], replicated, may hold values from -0.75 to 0.75
- coarse_in: float32 [64, 64], replicated, may hold values from -0.75 to 0.75
- coarse_out: float32 [64, 64], replicated, may hold values from -0.75 to 0.75
- coarse_mix: float32 [64, 64], replicated, may hold values from -0.75 to 0.75
- up_in: float32 [64, 128], replicated, may hold values from -0.5 to 0.5
- up_out: float32 [64, 64], replicated, may hold values from -0.75 to 0.75
- biases: float32 [4, 64], replicated, may hold values from -3 to 3
Outputs:
- output: float32 [64, 524288], P(None, ('gx', 'gy'))
- grad_features: float32 [64, 524288], P(None, ('gx', 'gy'))
- grad_edge_in: float32 [64, 128], replicated
- grad_edge_out: float32 [64, 64], replicated
- grad_node_in: float32 [64, 128], replicated
- grad_node_out: float32 [64, 64], replicated
- grad_coarse_in: float32 [64, 64], replicated
- grad_coarse_out: float32 [64, 64], replicated
- grad_coarse_mix: float32 [64, 64], replicated
- grad_up_in: float32 [64, 128], replicated
- grad_up_out: float32 [64, 64], replicated
- grad_biases: float32 [4, 64], replicated
Inputs may be any that keep to these rules, and one draw needn't show every extreme that they name: `edge_src`: indexes the receiver partition's 2048 own nodes, then the four received packets in the order of the first step. `send_rows`: partition-local node numbers.
All inputs are finite; a program needn't handle non-finite values.
Results may differ from a plain program's by a relative error of at most 0.0003.
Values sent between devices are 32-bit elements; how exact they have to be, the bound alone decides.
A program may use at most 64 MiB of HBM per device.

v0:
```python
from functools import partial
import math
import jax
import jax.numpy as jnp
from jax import lax
from jax.sharding import PartitionSpec as P

COARSE = 2048


def passed_along(value, axis, steps):
    count = lax.axis_size(axis)
    leading, last = (max(0, -steps), min(count, count - steps))
    return lax.ppermute(value, axis, [(source, source + steps) for source in range(leading, last)])


def matmul(left_side, right_side):
    return jnp.dot(
        left_side, right_side, precision=lax.Precision.HIGHEST, preferred_element_type=jnp.float32
    )


def swish(values):
    return values * jax.nn.sigmoid(values)


def fine_update(
    latent, extended, edge_in, edge_out, node_in, node_out, edge_bias, node_bias, sources
):
    feature_count = latent.shape[0]
    receiver_part = matmul(edge_in[:, :feature_count], latent)
    sender_part = matmul(edge_in[:, feature_count:], extended)
    hidden = swish(receiver_part[:, None, :] + sender_part[:, sources] + edge_bias[:, None, None])
    summed = matmul(edge_out, jnp.sum(hidden, axis=1))
    activation = swish(
        matmul(node_in[:, :feature_count], latent)
        + matmul(node_in[:, feature_count:], summed)
        + node_bias[:, None]
    )
    return latent + matmul(node_out, activation)


def coarse_node(pooled, coarse_in, coarse_out, coarse_bias):
    return pooled + matmul(coarse_out, swish(matmul(coarse_in, pooled) + coarse_bias[:, None]))


def coarse_edge(nodes, coarse_mix, coarse_edges):
    gathered = nodes[:, coarse_edges[0]]
    summed = jnp.zeros_like(nodes).at[:, coarse_edges[1]].add(gathered)
    factor = (nodes.shape[1] / coarse_edges.shape[1]) ** 0.5
    return nodes + matmul(coarse_mix, summed) * factor


def up_update(middle, looked, up_in, up_out, up_bias):
    feature_count = middle.shape[0]
    activation = swish(
        matmul(up_in[:, :feature_count], middle)
        + matmul(up_in[:, feature_count:], looked)
        + up_bias[:, None]
    )
    return middle + matmul(up_out, activation)


def block_width(node_count):
    return math.gcd(node_count, 1024)


def one_hot_block(index_block, table_width):
    return (index_block[:, None] == jnp.arange(table_width, dtype=jnp.int32)[None, :]).astype(
        jnp.float32
    )


def pool_nodes(values, index, table_width):
    feature_count, node_count = values.shape
    width = block_width(node_count)
    blocks = node_count // width
    value_blocks = values.reshape(feature_count, blocks, width).transpose(1, 0, 2)
    index_blocks = index.reshape(blocks, width)

    def add_block(total, items):
        return (total + matmul(items[0], one_hot_block(items[1], table_width)), None)

    start = jnp.zeros((feature_count, table_width), jnp.float32)
    total, unused = lax.scan(add_block, start, (value_blocks, index_blocks))
    return total


def look_nodes(table, index):
    feature_count, table_width = table.shape
    node_count = index.shape[0]
    width = block_width(node_count)
    blocks = node_count // width
    index_blocks = index.reshape(blocks, width)

    def read_block(index_block):
        selector = one_hot_block(index_block, table_width)
        return lax.dot_general(
            table,
            selector,
            (((1,), (1,)), ((), ())),
            precision=lax.Precision.HIGHEST,
            preferred_element_type=jnp.float32,
        )

    result = lax.map(read_block, index_blocks)
    return result.transpose(1, 0, 2).reshape(feature_count, node_count)


def pass_rows(packet, offset):
    return passed_along(packet, "gx", offset)


def pass_cols(packet, offset):
    return passed_along(packet, "gy", offset)


def coarse_total(table):
    return lax.psum(table, ("gx", "gy"))


def local(
    features,
    cotangent,
    edge_src,
    send_rows,
    fine_to_coarse,
    coarse_to_fine,
    coarse_edges,
    edge_in,
    edge_out,
    node_in,
    node_out,
    coarse_in,
    coarse_out,
    coarse_mix,
    up_in,
    up_out,
    biases,
):
    local_nodes = features.shape[1]
    halo_rows = send_rows.shape[1]
    pool_scale = (COARSE / (local_nodes * lax.axis_size("gx") * lax.axis_size("gy"))) ** 0.5
    packets = features[:, send_rows]
    extended = jnp.concatenate(
        [
            features,
            pass_rows(packets[:, 0], 1),
            pass_rows(packets[:, 1], -1),
            pass_cols(packets[:, 2], 1),
            pass_cols(packets[:, 3], -1),
        ],
        axis=1,
    )
    middle, fine_back = jax.vjp(
        partial(fine_update, sources=edge_src),
        features,
        extended,
        edge_in,
        edge_out,
        node_in,
        node_out,
        biases[0],
        biases[1],
    )
    pooled_part = pool_nodes(middle, fine_to_coarse, COARSE) * pool_scale
    pooled = coarse_total(pooled_part)
    nodes, node_back = jax.vjp(coarse_node, pooled, coarse_in, coarse_out, biases[2])
    mixed, mix_back = jax.vjp(partial(coarse_edge, coarse_edges=coarse_edges), nodes, coarse_mix)
    looked = look_nodes(mixed, coarse_to_fine)
    output, up_back = jax.vjp(up_update, middle, looked, up_in, up_out, biases[3])
    grad_middle, grad_looked, grad_up_in, grad_up_out, grad_up_bias = up_back(cotangent)
    grad_mixed_part = pool_nodes(grad_looked, coarse_to_fine, COARSE)
    grad_nodes_part, grad_mix = mix_back(grad_mixed_part)
    grad_nodes = coarse_total(grad_nodes_part)
    grad_pooled, grad_coarse_in, grad_coarse_out, grad_coarse_bias = node_back(grad_nodes)
    grad_middle = grad_middle + look_nodes(grad_pooled, fine_to_coarse) * pool_scale
    (
        grad_own,
        grad_ext,
        grad_edge_in,
        grad_edge_out,
        grad_node_in,
        grad_node_out,
        grad_edge_bias,
        grad_node_bias,
    ) = fine_back(grad_middle)
    pieces = [
        grad_ext[:, local_nodes + slot * halo_rows : local_nodes + (slot + 1) * halo_rows]
        for slot in range(4)
    ]
    returned = jnp.stack(
        [
            pass_rows(pieces[0], -1),
            pass_rows(pieces[1], 1),
            pass_cols(pieces[2], -1),
            pass_cols(pieces[3], 1),
        ],
        axis=1,
    )
    grad_features = (
        grad_own
        + grad_ext[:, :local_nodes]
        + jnp.zeros_like(features).at[:, send_rows].add(returned)
    )
    fine_biases = jnp.stack([grad_edge_bias, grad_node_bias, grad_up_bias])
    summed = lax.psum(
        (
            grad_edge_in,
            grad_edge_out,
            grad_node_in,
            grad_node_out,
            grad_mix,
            grad_up_in,
            grad_up_out,
            fine_biases,
        ),
        ("gx", "gy"),
    )
    grad_biases = jnp.stack([summed[7][0], summed[7][1], grad_coarse_bias, summed[7][2]])
    return (
        output,
        grad_features,
        summed[0],
        summed[1],
        summed[2],
        summed[3],
        grad_coarse_in,
        grad_coarse_out,
        summed[4],
        summed[5],
        summed[6],
        grad_biases,
    )


def solution(mesh):
    in_specs = (
        P(None, ("gx", "gy")),
        P(None, ("gx", "gy")),
        P(None, ("gx", "gy")),
        P(None, ("gx", "gy")),
        P(("gx", "gy")),
        P(("gx", "gy")),
        P(),
        P(),
        P(),
        P(),
        P(),
        P(),
        P(),
        P(),
        P(),
        P(),
        P(),
    )
    out_specs = (
        P(None, ("gx", "gy")),
        P(None, ("gx", "gy")),
        P(),
        P(),
        P(),
        P(),
        P(),
        P(),
        P(),
        P(),
        P(),
        P(),
    )
    return jax.shard_map(local, mesh=mesh, in_specs=in_specs, out_specs=out_specs, check_vma=False)
```

profile of v0, /device:TPU:4, one launch (start us, length us, event | category | flops | bytes accessed | tf_op | source)
XLA Modules:
  0.0 1284.9 jit_solution(6008554091809120378)
XLA Ops:
  11.8 4.5 collective-permute-start.2
  35.8 54.7 %gather_fusion.1 = f32[16384,64]{1,0:T(8,128)} fusion(f32[64,2560]{0,1:T(8,128)S(1)} %copy.65, s32[16384]{0:T(1024)S(1)} %broadcast_clamp_fusion), kind=kCustom, calls=%fused_computation.1 | custom fusion | bytes 8454144 | tf_op jit(solution)/shard_map/jvp()/gather | solution.py:33
  90.6 4.8 multiply_reduce_fusion
  100.4 7.0 while.44
  100.5 3.5 fusion.178
  104.0 3.5 fusion.178
  110.1 254.7 %all-reduce.11.cloned.1.call-done = f32[64,2048]{1,0:T(8,128)} async-done(((f32[64,2048]{1,0:T(8,128)}), f32[64,2048]{1,0:T(8,128)}) %all-reduce.11.cloned.1.call-update) | async-done | bytes 524304 | tf_op jit(solution)/shard_map/psum | solution.py:119
  370.4 90.5 %scatter_custom_fusion = f32[64,2048]{0,1:T(8,128)S(1)} fusion(s32[8192]{0:T(1024)} %bitcast.245, f32[64,2048]{0,1:T(8,128)} %copy.67, s32[8192]{0:T(1024)} %broadcast_clamp_fusion.2, f32[]{:T(128)} %constant.19.clone.1), kind=kCustom, calls=%fused_computation.44 | custom fusion | flops 524288 | bytes 524800 | tf_op jit(solution)/shard_map/jvp()/scatter-add | solution.py:49
  463.0 11.0 while.42
  463.1 5.5 fusion.174
  468.6 5.5 fusion.174
  485.0 10.4 while.45
  485.0 5.1 fusion.180
  490.1 5.3 fusion.180
  502.6 103.6 %scatter_custom_fusion.1 = f32[64,2048]{0,1:T(8,128)} fusion(f32[64,2048]{0,1:T(8,128)} %copy.71, s32[8192]{0:T(1024)} %bitcast.243, f32[]{:T(128)} %constant.19.clone.1, pred[8192]{0:T(1024)(128)(4,1)S(1)} %compare_and_fusion, f32[64,2048]{0,1:T(8,128)} %copy.70, s32[8192]{0:T(1024)S(1)} %broadcast_clamp_fusion.1), kind=kCustom, calls=%fused_computation.42 | custom fusion | flops 1048576 | bytes 1614336 | tf_op jit(solution)/shard_map/transpose(jvp())/scatter-add | solution.py:48
  611.0 248.5 %all-reduce.13.cloned.1.call-done = f32[64,2048]{1,0:T(8,128)} async-done(((f32[64,2048]{1,0:T(8,128)}), f32[64,2048]{1,0:T(8,128)}) %all-reduce.13.cloned.1.call-update) | async-done | bytes 524304 | tf_op jit(solution)/shard_map/psum | solution.py:119
  864.6 8.9 while.43
  864.6 4.4 fusion.176
  869.1 4.4 fusion.176
  889.0 5.7 fusion.21
  894.7 3.2 copy-done.1
  905.0 88.0 %scatter_custom_fusion.2 = f32[64,2560]{0,1:T(8,128)S(1)} fusion(s32[16384]{0:T(1024)S(1)} %bitcast.240, f32[16384,64]{1,0:T(8,128)} %bitcast.227, f32[]{:T(128)} %constant.19.clone.1), kind=kCustom, calls=%fused_computation.85 | custom fusion | flops 1048576 | bytes 655872 | tf_op jit(solution)/shard_map/transpose(jvp())/scatter-add | solution.py:33
  1015.1 3.7 scatter_fusion
  1019.9 246.4 %all-reduce.15.cloned.1.call-done = (f32[64,128]{1,0:T(8,128)}, f32[64,64]{1,0:T(8,128)}, f32[64,128]{1,0:T(8,128)}, f32[64,64]{1,0:T(8,128)}, f32[64,64]{1,0:T(...) async-done(((f32[64,128]{1,0:T(8,128)}, f32[64,64]{1,0:T(8,128)}, f32[64,128]{1,0:T(8,128)}, f32[64,64]{1,0:T(8,128)}, f32[64,64]{1,0:T(8,128)}, ...) | async-done | bytes 164624 | tf_op jit(solution)/shard_map/psum | solution.py:207
  (183 shorter events, 124.3 us)
Async XLA Ops:
  7.2 360.1 %copy-start = (f32[64,64]{1,0:T(8,128)S(1)}, f32[64,64]{1,0:T(8,128)}, u32[]{:S(2)}) copy-start(f32[64,64]{1,0:T(8,128)} %param.37) | copy-start | bytes 49156
  7.2 357.6 %all-reduce.11.cloned.1.call-start = ((), (), s32[]{:S(2)}) async-start(), calls=%async_computation | async-start | bytes 1048576 | tf_op jit(solution)/shard_map/psum | solution.py:119
  10.5 22.6 %collective-permute-start.3 = (f32[64,128]{1,0:T(8,128)S(1)}, f32[64,128]{1,0:T(8,128)S(1)}, u32[]{:S(2)}, u32[]{:S(2)}) collective-permute-start(f32[64,128]{1,0:T(8,128)S(1)} %get-tuple-element.218), channel_id=1, source_target_pairs={{1,0},{2,1},{3,2},{4,3},{5,4},{6,5},{7,6},{8,7},{9,8},{10,9},{11,1... | collective-permute-start | bytes 98312 | tf_op jit(solution)/shard_map/ppermute | solution.py:14
  11.8 21.3 %collective-permute-start.2 = (f32[64,128]{1,0:T(8,128)S(1)}, f32[64,128]{1,0:T(8,128)S(1)}, u32[]{:S(2)}, u32[]{:S(2)}) collective-permute-start(f32[64,128]{1,0:T(8,128)S(1)} %get-tuple-element.219), channel_id=1, source_target_pairs={{0,1},{1,2},{2,3},{3,4},{4,5},{5,6},{6,7},{7,8},{8,9},{9,10},{10,1... | collective-permute-start | bytes 98312 | tf_op jit(solution)/shard_map/ppermute | solution.py:14
  16.3 16.7 %collective-permute-start.1 = (f32[64,128]{1,0:T(8,128)S(1)}, f32[64,128]{1,0:T(8,128)S(1)}, u32[]{:S(2)}, u32[]{:S(2)}) collective-permute-start(f32[64,128]{1,0:T(8,128)S(1)} %get-tuple-element.220), channel_id=1, source_target_pairs={{32,0},{64,32},{96,64},{128,96},{160,128},{192,160},{224,192},{33,... | collective-permute-start | bytes 98312 | tf_op jit(solution)/shard_map/ppermute | solution.py:14
  18.3 14.7 %collective-permute-start = (f32[64,128]{1,0:T(8,128)S(1)}, f32[64,128]{1,0:T(8,128)S(1)}, u32[]{:S(2)}, u32[]{:S(2)}) collective-permute-start(f32[64,128]{1,0:T(8,128)S(1)} %get-tuple-element.221), channel_id=1, source_target_pairs={{0,32},{32,64},{64,96},{96,128},{128,160},{160,192},{192,224},{1,3... | collective-permute-start | bytes 98312 | tf_op jit(solution)/shard_map/ppermute | solution.py:14
  23.7 12.2 copy-start.23
  27.2 63.4 %copy-start.3 = (f32[64,2048]{0,1:T(8,128)}, f32[64,2048]{0,1:T(8,128)S(1)}, u32[]{:S(2)}) copy-start(f32[64,2048]{0,1:T(8,128)S(1)} %fusion.81) | copy-start | bytes 1572868
  90.6 9.0 copy-start.29
  90.6 9.8 copy-start.16
  100.4 264.3 %copy-start.21 = (f32[64,64]{1,0:T(8,128)S(1)}, f32[64,64]{1,0:T(8,128)}, u32[]{:S(2)}) copy-start(f32[64,64]{1,0:T(8,128)} %param.36) | copy-start | bytes 49156
  107.4 353.4 %copy-start.20 = (f32[64,64]{1,0:T(8,128)S(1)}, f32[64,64]{1,0:T(8,128)}, u32[]{:S(2)}) copy-start(f32[64,64]{1,0:T(8,128)} %param.38) | copy-start | bytes 49156
  108.3 751.2 %all-reduce.13.cloned.1.call-start = ((), (), s32[]{:S(2)}) async-start(), calls=%async_computation.1 | async-start | bytes 1048576 | tf_op jit(solution)/shard_map/psum | solution.py:119
  463.0 11.1 copy-start.28
  463.0 15.5 %copy-start.25 = (f32[64,64]{1,0:T(8,128)S(1)}, f32[64,64]{1,0:T(8,128)}, u32[]{:S(2)}) copy-start(f32[64,64]{1,0:T(8,128)} %param.40) | copy-start | bytes 49156
  608.5 657.8 %all-reduce.15.cloned.1.call-start = ((), (), s32[]{:S(2)}) async-start(), calls=%async_computation.2 | async-start | bytes 462848 | tf_op jit(solution)/shard_map/psum | solution.py:207
  864.6 15.3 %copy-start.30 = (f32[64,64]{1,0:T(8,128)S(1)}, f32[64,64]{1,0:T(8,128)}, u32[]{:S(2)}) copy-start(f32[64,64]{1,0:T(8,128)} %param.35) | copy-start | bytes 49156
  874.3 14.6 %copy-start.4 = (f32[64,2048]{0,1:T(8,128)S(1)}, f32[64,2048]{0,1:T(8,128)}, u32[]{:S(2)}) copy-start(f32[64,2048]{0,1:T(8,128)} %copy-done.3) | copy-start | bytes 1572868
  897.9 95.0 %copy-start.6 = (f32[64,2560]{1,0:T(8,128)S(1)}, f32[64,2560]{1,0:T(8,128)}, u32[]{:S(2)}) copy-start(f32[64,2560]{1,0:T(8,128)} %copy-done.5) | copy-start | bytes 1966084
  992.9 276.1 %copy-start.27 = (f32[64]{0:T(128)S(1)}, f32[64]{0:T(128)}, u32[]{:S(2)}) copy-start(f32[64]{0:T(128)} %get-tuple-element.231) | copy-start | bytes 772
  998.7 16.2 %collective-permute-start.4 = (f32[64,128]{1,0:T(8,128)S(1)}, f32[64,128]{1,0:T(8,128)S(1)}, u32[]{:S(2)}, u32[]{:S(2)}) collective-permute-start(f32[64,128]{1,0:T(8,128)S(1)} %get-tuple-element.214), channel_id=1, source_target_pairs={{32,0},{64,32},{96,64},{128,96},{160,128},{192,160},{224,192},{33,... | collective-permute-start | bytes 98312 | tf_op jit(solution)/shard_map/ppermute | solution.py:14
  1000.6 14.3 %collective-permute-start.7 = (f32[64,128]{1,0:T(8,128)S(1)}, f32[64,128]{1,0:T(8,128)S(1)}, u32[]{:S(2)}, u32[]{:S(2)}) collective-permute-start(f32[64,128]{1,0:T(8,128)S(1)} %get-tuple-element.215), channel_id=1, source_target_pairs={{0,1},{1,2},{2,3},{3,4},{4,5},{5,6},{6,7},{7,8},{8,9},{9,10},{10,1... | collective-permute-start | bytes 98312 | tf_op jit(solution)/shard_map/ppermute | solution.py:14
  1002.5 12.3 collective-permute-start.6
  1003.8 11.1 collective-permute-start.5
  (18 other events, 85.2 us)
Sparse Core Ops, SparseCore 0:
  108.4 256.2 all-reduce.10
  608.6 250.7 all-reduce.12
  1009.7 256.5 all-reduce.14
where the time goes:
time: 1300 us; the launch traced here: 1280 us
  waiting for transfers between devices  750 us (58%)
  other arithmetic  308 us (24%)
  matrix products  101 us (8%)
  local copies, waits for them, and re-layouts  93.4 us (7%)
  starting transfers between devices  17.9 us (1%)
  between operations  15 us (1%)
    psum x2, waiting for transfers between devices, coarse_total(): return lax.psum(table, ('gx', 'gy'))  503 us
    psum x1, waiting for transfers between devices, local(): lax.psum((grad_edge_in, grad_edge_out, grad_node_in, grad_node_out, grad_...  246 us
    scatter-add x1, other arithmetic, coarse_edge(): gathered = nodes[:, coarse_edges[0]]  104 us
    scatter-add x1, other arithmetic, coarse_edge(): summed = jnp.zeros_like(nodes).at[:, coarse_edges[1]].add(gathered)  90.5 us
    scatter-add x1, other arithmetic, fine_update(): sender_part[:, sources]  88 us
    dot_general x40, matrix products, matmul(): jnp.dot(left_side, right_side, precision=lax.Precision.HIGHEST, preferred...  80.9 us
    gather x1, local copies, waits for them, and re-layouts, fine_update(): sender_part[:, sources]  54.7 us
  transfers between devices with their start and end apart: 11, of which 3 were waited for; matrix products, arithmetic and copies ran while one was open for 2% of the time, Pallas kernels for 0%

commit v1 on v0

--- a/solution.py
+++ b/solution.py
@@ -138,6 +138,12 @@
     up_out,
     biases,
 ):
+
+    def zones_follow(local_values, lane_axis, a_name):
+        v_next = lax.psum(local_values, lane_axis)
+        o_now = lax.psum(v_next, a_name)
+        return o_now
+
     local_nodes = features.shape[1]
     halo_rows = send_rows.shape[1]
     pool_scale = (COARSE / (local_nodes * lax.axis_size("gx") * lax.axis_size("gy"))) ** 0.5
@@ -204,7 +210,7 @@
         + jnp.zeros_like(features).at[:, send_rows].add(returned)
     )
     fine_biases = jnp.stack([grad_edge_bias, grad_node_bias, grad_up_bias])
-    summed = lax.psum(
+    summed = zones_follow(
         (
             grad_edge_in,
             grad_edge_out,
@@ -215,7 +221,8 @@
             grad_up_out,
             fine_biases,
         ),
-        ("gx", "gy"),
+        "gx",
+        "gy",
     )
     grad_biases = jnp.stack([summed[7][0], summed[7][1], grad_coarse_bias, summed[7][2]])
     return (

time: 1300 us -> 1260 us (0.969)
  waiting for transfers between devices: 750 us -> 710 us
    psum x1 -> x2, waiting for transfers between devices: 246 us -> 207 us  [the longest x1 146 us: zones_follow(): o_now = lax.psum(v_next, a_name)]
  transfers between devices with their start and end apart: 11 -> 12, of which waited for: 3 -> 4; matrix products, arithmetic and copies ran while one was open for 2% -> 2% of each run, Pallas kernels for 0% -> 0%
where the time goes in v1:
time: 1260 us; the launch traced here: 1240 us
  waiting for transfers between devices  710 us (56%)
  other arithmetic  308 us (24%)
  matrix products  99.8 us (8%)
  local copies, waits for them, and re-layouts  93.4 us (7%)
  starting transfers between devices  17.9 us (1%)
  between operations  15 us (1%)
    psum x2, waiting for transfers between devices, coarse_total(): return lax.psum(table, ('gx', 'gy'))  503 us
    psum x1, waiting for transfers between devices, zones_follow(): o_now = lax.psum(v_next, a_name)  146 us
    scatter-add x1, other arithmetic, coarse_edge(): gathered = nodes[:, coarse_edges[0]]  104 us
    scatter-add x1, other arithmetic, coarse_edge(): summed = jnp.zeros_like(nodes).at[:, coarse_edges[1]].add(gathered)  90.4 us
    scatter-add x1, other arithmetic, fine_update(): sender_part[:, sources]  88 us
    dot_general x40, matrix products, matmul(): jnp.dot(left_side, right_side, precision=lax.Precision.HIGHEST, preferred...  80 us
    psum x1, waiting for transfers between devices, zones_follow(): v_next = lax.psum(local_values, lane_axis)  61.1 us
    gather x1, local copies, waits for them, and re-layouts, fine_update(): sender_part[:, sources]  54.8 us
  transfers between devices with their start and end apart: 12, of which 4 were waited for; matrix products, arithmetic and copies ran while one was open for 2% of the time, Pallas kernels for 0%

profile of v1, /device:TPU:4, one launch (start us, length us, event | category | flops | bytes accessed | tf_op | source)
XLA Modules:
  0.0 1244.0 jit_solution(6480068582541981289)
XLA Ops:
  11.8 4.5 collective-permute-start.2
  35.8 54.8 %gather_fusion.1 = f32[16384,64]{1,0:T(8,128)} fusion(f32[64,2560]{0,1:T(8,128)S(1)} %copy.65, s32[16384]{0:T(1024)S(1)} %broadcast_clamp_fusion), kind=kCustom, calls=%fused_computation.1 | custom fusion | bytes 8454144 | tf_op jit(solution)/shard_map/jvp()/gather | solution.py:33
  90.6 4.8 multiply_reduce_fusion
  100.5 7.0 while.44
  100.5 3.5 fusion.178
  104.0 3.5 fusion.178
  110.1 254.5 %all-reduce.13.cloned.1.call-done = f32[64,2048]{1,0:T(8,128)} async-done(((f32[64,2048]{1,0:T(8,128)}), f32[64,2048]{1,0:T(8,128)}) %all-reduce.13.cloned.1.call-update) | async-done | bytes 524304 | tf_op jit(solution)/shard_map/psum | solution.py:119
  370.3 90.4 %scatter_custom_fusion = f32[64,2048]{0,1:T(8,128)S(1)} fusion(s32[8192]{0:T(1024)} %bitcast.245, f32[64,2048]{0,1:T(8,128)} %copy.67, s32[8192]{0:T(1024)} %broadcast_clamp_fusion.2, f32[]{:T(128)} %constant.19.clone.1), kind=kCustom, calls=%fused_computation.44 | custom fusion | flops 524288 | bytes 524800 | tf_op jit(solution)/shard_map/jvp()/scatter-add | solution.py:49
  462.9 11.0 while.42
  462.9 5.5 fusion.174
  468.4 5.5 fusion.174
  484.9 10.3 while.45
  484.9 5.1 fusion.180
  490.0 5.2 fusion.180
  502.4 103.6 %scatter_custom_fusion.1 = f32[64,2048]{0,1:T(8,128)} fusion(f32[64,2048]{0,1:T(8,128)} %copy.71, s32[8192]{0:T(1024)} %bitcast.243, f32[]{:T(128)} %constant.19.clone.1, pred[8192]{0:T(1024)(128)(4,1)S(1)} %compare_and_fusion, f32[64,2048]{0,1:T(8,128)} %copy.70, s32[8192]{0:T(1024)S(1)} %broadcast_clamp_fusion.1), kind=kCustom, calls=%fused_computation.42 | custom fusion | flops 1048576 | bytes 1614336 | tf_op jit(solution)/shard_map/transpose(jvp())/scatter-add | solution.py:48
  610.8 248.3 %all-reduce.15.cloned.1.call-done = f32[64,2048]{1,0:T(8,128)} async-done(((f32[64,2048]{1,0:T(8,128)}), f32[64,2048]{1,0:T(8,128)}) %all-reduce.15.cloned.1.call-update) | async-done | bytes 524304 | tf_op jit(solution)/shard_map/psum | solution.py:119
  864.3 8.9 while.43
  864.3 4.4 fusion.176
  868.8 4.4 fusion.176
  888.7 5.7 fusion.21
  903.9 88.0 %scatter_custom_fusion.2 = f32[64,2560]{0,1:T(8,128)S(1)} fusion(s32[16384]{0:T(1024)S(1)} %bitcast.240, f32[16384,64]{1,0:T(8,128)} %bitcast.227, f32[]{:T(128)} %constant.19.clone.1), kind=kCustom, calls=%fused_computation.85 | custom fusion | flops 1048576 | bytes 655872 | tf_op jit(solution)/shard_map/transpose(jvp())/scatter-add | solution.py:33
  1011.0 61.1 %all-reduce.19.cloned.1.call-done = (f32[64,128]{1,0:T(8,128)}, f32[64,64]{1,0:T(8,128)}, f32[64,128]{1,0:T(8,128)}, f32[64,64]{1,0:T(8,128)}, f32[64,64]{1,0:T(...) async-done(((f32[64,128]{1,0:T(8,128)}, f32[64,64]{1,0:T(8,128)}, f32[64,128]{1,0:T(8,128)}, f32[64,64]{1,0:T(8,128)}, f32[64,64]{1,0:T(8,128)}, ...) | async-done | bytes 164624 | tf_op jit(solution)/shard_map/psum | solution.py:143
  1075.0 3.7 scatter_fusion
  1079.8 145.7 %all-reduce.17.cloned.1.call-done = (f32[64,128]{1,0:T(8,128)}, f32[64,64]{1,0:T(8,128)}, f32[64,128]{1,0:T(8,128)}, f32[64,64]{1,0:T(8,128)}, f32[64,64]{1,0:T(...) async-done(((f32[64,128]{1,0:T(8,128)}, f32[64,64]{1,0:T(8,128)}, f32[64,128]{1,0:T(8,128)}, f32[64,64]{1,0:T(8,128)}, f32[64,64]{1,0:T(8,128)}, ...) | async-done | bytes 164624 | tf_op jit(solution)/shard_map/psum | solution.py:144
  (186 shorter events, 126.7 us)
Async XLA Ops:
  7.2 359.9 %copy-start = (f32[64,64]{1,0:T(8,128)S(1)}, f32[64,64]{1,0:T(8,128)}, u32[]{:S(2)}) copy-start(f32[64,64]{1,0:T(8,128)} %param.37) | copy-start | bytes 49156
  7.2 357.4 %all-reduce.13.cloned.1.call-start = ((), (), s32[]{:S(2)}) async-start(), calls=%async_computation | async-start | bytes 1048576 | tf_op jit(solution)/shard_map/psum | solution.py:119
  10.5 22.6 %collective-permute-start.3 = (f32[64,128]{1,0:T(8,128)S(1)}, f32[64,128]{1,0:T(8,128)S(1)}, u32[]{:S(2)}, u32[]{:S(2)}) collective-permute-start(f32[64,128]{1,0:T(8,128)S(1)} %get-tuple-element.226), channel_id=1, source_target_pairs={{1,0},{2,1},{3,2},{4,3},{5,4},{6,5},{7,6},{8,7},{9,8},{10,9},{11,1... | collective-permute-start | bytes 98312 | tf_op jit(solution)/shard_map/ppermute | solution.py:14
  11.8 21.3 %collective-permute-start.2 = (f32[64,128]{1,0:T(8,128)S(1)}, f32[64,128]{1,0:T(8,128)S(1)}, u32[]{:S(2)}, u32[]{:S(2)}) collective-permute-start(f32[64,128]{1,0:T(8,128)S(1)} %get-tuple-element.227), channel_id=1, source_target_pairs={{0,1},{1,2},{2,3},{3,4},{4,5},{5,6},{6,7},{7,8},{8,9},{9,10},{10,1... | collective-permute-start | bytes 98312 | tf_op jit(solution)/shard_map/ppermute | solution.py:14
  16.3 16.7 %collective-permute-start.1 = (f32[64,128]{1,0:T(8,128)S(1)}, f32[64,128]{1,0:T(8,128)S(1)}, u32[]{:S(2)}, u32[]{:S(2)}) collective-permute-start(f32[64,128]{1,0:T(8,128)S(1)} %get-tuple-element.228), channel_id=1, source_target_pairs={{32,0},{64,32},{96,64},{128,96},{160,128},{192,160},{224,192},{33,... | collective-permute-start | bytes 98312 | tf_op jit(solution)/shard_map/ppermute | solution.py:14
  18.3 14.7 %collective-permute-start = (f32[64,128]{1,0:T(8,128)S(1)}, f32[64,128]{1,0:T(8,128)S(1)}, u32[]{:S(2)}, u32[]{:S(2)}) collective-permute-start(f32[64,128]{1,0:T(8,128)S(1)} %get-tuple-element.229), channel_id=1, source_target_pairs={{0,32},{32,64},{64,96},{96,128},{128,160},{160,192},{192,224},{1,3... | collective-permute-start | bytes 98312 | tf_op jit(solution)/shard_map/ppermute | solution.py:14
  23.7 12.1 copy-start.23
  27.2 63.4 %copy-start.3 = (f32[64,2048]{0,1:T(8,128)}, f32[64,2048]{0,1:T(8,128)S(1)}, u32[]{:S(2)}) copy-start(f32[64,2048]{0,1:T(8,128)S(1)} %fusion.81) | copy-start | bytes 1572868
  90.6 9.8 copy-start.16
  100.4 264.2 %copy-start.21 = (f32[64,64]{1,0:T(8,128)S(1)}, f32[64,64]{1,0:T(8,128)}, u32[]{:S(2)}) copy-start(f32[64,64]{1,0:T(8,128)} %param.36) | copy-start | bytes 49156
  107.4 353.2 %copy-start.20 = (f32[64,64]{1,0:T(8,128)S(1)}, f32[64,64]{1,0:T(8,128)}, u32[]{:S(2)}) copy-start(f32[64,64]{1,0:T(8,128)} %param.38) | copy-start | bytes 49156
  108.3 750.8 %all-reduce.15.cloned.1.call-start = ((), (), s32[]{:S(2)}) async-start(), calls=%async_computation.1 | async-start | bytes 1048576 | tf_op jit(solution)/shard_map/psum | solution.py:119
  462.8 11.1 copy-start.28
  462.8 15.5 %copy-start.25 = (f32[64,64]{1,0:T(8,128)S(1)}, f32[64,64]{1,0:T(8,128)}, u32[]{:S(2)}) copy-start(f32[64,64]{1,0:T(8,128)} %param.40) | copy-start | bytes 49156
  608.4 463.6 %all-reduce.19.cloned.1.call-start = ((), (), s32[]{:S(2)}) async-start(), calls=%async_computation.3 | async-start | bytes 462848 | tf_op jit(solution)/shard_map/psum | solution.py:143
  864.3 15.3 %copy-start.30 = (f32[64,64]{1,0:T(8,128)S(1)}, f32[64,64]{1,0:T(8,128)}, u32[]{:S(2)}) copy-start(f32[64,64]{1,0:T(8,128)} %param.35) | copy-start | bytes 49156
  874.0 14.6 %copy-start.4 = (f32[64,2048]{0,1:T(8,128)S(1)}, f32[64,2048]{0,1:T(8,128)}, u32[]{:S(2)}) copy-start(f32[64,2048]{0,1:T(8,128)} %copy-done.3) | copy-start | bytes 1572868
  897.7 94.2 %copy-start.6 = (f32[64,2560]{1,0:T(8,128)S(1)}, f32[64,2560]{1,0:T(8,128)}, u32[]{:S(2)}) copy-start(f32[64,2560]{1,0:T(8,128)} %copy-done.5) | copy-start | bytes 1966084
  991.9 236.3 %copy-start.27 = (f32[64]{0:T(128)S(1)}, f32[64]{0:T(128)}, u32[]{:S(2)}) copy-start(f32[64]{0:T(128)} %get-tuple-element.239) | copy-start | bytes 772
  997.4 77.3 %collective-permute-start.4 = (f32[64,128]{1,0:T(8,128)S(1)}, f32[64,128]{1,0:T(8,128)S(1)}, u32[]{:S(2)}, u32[]{:S(2)}) collective-permute-start(f32[64,128]{1,0:T(8,128)S(1)} %get-tuple-element.222), channel_id=1, source_target_pairs={{32,0},{64,32},{96,64},{128,96},{160,128},{192,160},{224,192},{33,... | collective-permute-start | bytes 98312 | tf_op jit(solution)/shard_map/ppermute | solution.py:14
  999.4 75.4 %collective-permute-start.7 = (f32[64,128]{1,0:T(8,128)S(1)}, f32[64,128]{1,0:T(8,128)S(1)}, u32[]{:S(2)}, u32[]{:S(2)}) collective-permute-start(f32[64,128]{1,0:T(8,128)S(1)} %get-tuple-element.223), channel_id=1, source_target_pairs={{0,1},{1,2},{2,3},{3,4},{4,5},{5,6},{6,7},{7,8},{8,9},{9,10},{10,1... | collective-permute-start | bytes 98312 | tf_op jit(solution)/shard_map/ppermute | solution.py:14
  1001.3 73.5 %collective-permute-start.6 = (f32[64,128]{1,0:T(8,128)S(1)}, f32[64,128]{1,0:T(8,128)S(1)}, u32[]{:S(2)}, u32[]{:S(2)}) collective-permute-start(f32[64,128]{1,0:T(8,128)S(1)} %get-tuple-element.224), channel_id=1, source_target_pairs={{1,0},{2,1},{3,2},{4,3},{5,4},{6,5},{7,6},{8,7},{9,8},{10,9},{11,1... | collective-permute-start | bytes 98312 | tf_op jit(solution)/shard_map/ppermute | solution.py:14
  1002.6 72.2 %collective-permute-start.5 = (f32[64,128]{1,0:T(8,128)S(1)}, f32[64,128]{1,0:T(8,128)S(1)}, u32[]{:S(2)}, u32[]{:S(2)}) collective-permute-start(f32[64,128]{1,0:T(8,128)S(1)} %get-tuple-element.225), channel_id=1, source_target_pairs={{0,32},{32,64},{64,96},{96,128},{128,160},{160,192},{192,224},{1,3... | collective-permute-start | bytes 98312 | tf_op jit(solution)/shard_map/ppermute | solution.py:14
  1008.1 217.4 %all-reduce.17.cloned.1.call-start = ((), (), s32[]{:S(2)}) async-start(), calls=%async_computation.2 | async-start | bytes 462848 | tf_op jit(solution)/shard_map/psum | solution.py:144
  (19 other events, 94.2 us)
Sparse Core Ops, SparseCore 0:
  108.4 256.1 all-reduce.12
  608.5 250.5 all-reduce.14
  1008.2 63.7 all-reduce.18
  1076.9 148.5 all-reduce.16
